TPU v7x, 256 devices: a whole 4x4x8 slice. The times are simulated.
256 devices in a mesh: gx: 8 (over z_lo, x), gy: 32 (over z_hi, y, core).
Axes of the slice: x: 4, y: 4, z: 8 (z_hi: 4, z_lo: 2; z = z_hi * 2 + z_lo), core: 2. Of those that a mesh axis runs over, the one named last changes fastest.
Arguments:
- velocity: float32 [3, 32, 128, 4096], P(None, None, 'gx', 'gy'), may hold values from -6 to 6
- viscosity: float32 [32, 128, 4096], P(None, 'gx', 'gy'), may hold values from 0.02 to 0.12
- marker_cells: int32 [8192, 3, 128], P(('gx', 'gy')), may hold values from 0 to 4095, as said below
- marker_offset: float32 [8192, 3, 128], P(('gx', 'gy')), may hold values from 0 to 1
- marker_force: float32 [8192, 3, 128], P(('gx', 'gy')), may hold values from -24 to 24
Outputs:
- fluid_velocity: float32 [3, 32, 128, 4096], P(None, None, 'gx', 'gy')
- marker_velocity: float32 [8192, 3, 128], P(('gx', 'gy'))
Inputs may be any that keep to these rules, and one draw needn't show every extreme that they name: `marker_cells`: within one block every marker's x lies in [i * 16, (i + 1) * 16) where i is the gx index of the device holding the block, every marker's y lies in one range [j * 128, (j + 1) * 128), and z lies in [1, 29]. One device holds at most 2 blocks whose y range is one given j, and in every gx column some j receives exactly 2 blocks from every device of that column.
All inputs are finite; a program needn't handle non-finite values.
Results may differ from a plain program's by a relative error of at most 0.0003.
The roundings to bfloat16 on the way count: a program that leaves them out, or rounds other values in their place, can miss the bound.
Values may be sent and summed in bfloat16 or wider, within the bound.
A program may use at most 128 MiB of HBM per device.

v0:
```python
import jax
import jax.numpy as jnp
from jax import lax
from jax.sharding import PartitionSpec as P

CAP = 2
OFFSETS = (-1, 0, 1, 2)
group_slots = 4


def padded_2(array, sides, width):
    for axis, dim in sides:
        count, length = (lax.axis_size(axis), array.shape[dim])
        up = [(i, (i + 1) % count) for i in range(count)]
        down = [(j, i) for i, j in up]
        last = lax.slice_in_dim(array, length - width, length, axis=dim)
        first = lax.slice_in_dim(array, 0, width, axis=dim)
        before = lax.ppermute(last, axis, up)
        after = lax.ppermute(first, axis, down)
        array = jnp.concatenate([before, array, after], axis=dim)
    return array


def peskin_weight(distance):
    magnitude = jnp.abs(distance)
    inner = (
        3.0 - 2.0 * magnitude + jnp.sqrt(1.0 + 4.0 * magnitude - 4.0 * magnitude * magnitude)
    ) / 8.0
    outer = (
        5.0 - 2.0 * magnitude - jnp.sqrt(-7.0 + 12.0 * magnitude - 4.0 * magnitude * magnitude)
    ) / 8.0
    return jnp.where(magnitude < 1.0, inner, outer)


def stencil_matrix(cells, offsets, first_row, rows):
    line = lax.broadcasted_iota(jnp.int32, (rows, cells.shape[0]), 0)
    relative = cells - first_row
    matrix = jnp.zeros((rows, cells.shape[0]), jnp.float32)
    for shift_value in OFFSETS:
        weight_row = peskin_weight(shift_value - offsets)
        matrix = matrix + jnp.where(
            line == relative[None, :] + shift_value, weight_row[None, :], 0.0
        )
    return matrix


def slot_matrices(group, x_first, y_first, x_rows, y_rows, depth):
    flat = jnp.moveaxis(group, 1, 0).reshape(group.shape[1], -1)
    cells = flat[0:3].astype(jnp.int32)
    x_matrix = stencil_matrix(cells[0], flat[3], x_first, x_rows)
    y_matrix = stencil_matrix(cells[1], flat[4], y_first, y_rows).astype(jnp.bfloat16)
    z_matrix = stencil_matrix(cells[2], flat[5], 0, depth)
    return (flat[6:9], x_matrix, y_matrix, z_matrix)


def fold_ghosts(padded, axis, size):
    core = lax.slice_in_dim(padded, 4, size + 4, axis=axis)
    low_part = lax.slice_in_dim(padded, 0, 2, axis=axis)
    high_part = lax.slice_in_dim(padded, size + 6, size + 8, axis=axis)
    head = lax.slice_in_dim(core, 0, 2, axis=axis) + low_part
    middle = lax.slice_in_dim(core, 2, size - 2, axis=axis)
    tail = lax.slice_in_dim(core, size - 2, size, axis=axis) + high_part
    return jnp.concatenate([head, middle, tail], axis=axis)


def relax(padded_field, padded_visc):
    center_field = padded_field[:, :, 1:-1, 1:-1]
    center_visc = padded_visc[:, :, 1:-1, 1:-1]

    def face(neighbor_field, neighbor_visc):
        return 0.5 * (center_visc + neighbor_visc) * (neighbor_field - center_field)

    total = face(padded_field[:, :, :-2, 1:-1], padded_visc[:, :, :-2, 1:-1])
    total = total + face(padded_field[:, :, 2:, 1:-1], padded_visc[:, :, 2:, 1:-1])
    total = total + face(padded_field[:, :, 1:-1, :-2], padded_visc[:, :, 1:-1, :-2])
    total = total + face(padded_field[:, :, 1:-1, 2:], padded_visc[:, :, 1:-1, 2:])
    vertical = center_field[:, 1:] - center_field[:, :-1]
    vertical = 0.5 * (center_visc[:, 1:] + center_visc[:, :-1]) * vertical
    zeros_layer = jnp.zeros_like(vertical[:, :1])
    z_term = jnp.concatenate([vertical, zeros_layer], axis=1) - jnp.concatenate(
        [zeros_layer, vertical], axis=1
    )
    return center_field + (total + z_term)


def body(velocity, viscosity, marker_cells, marker_offset, marker_force):
    depth = velocity.shape[1]
    width_x = velocity.shape[2]
    width_y = velocity.shape[3]
    markers = marker_cells.shape[2]
    column_size = lax.axis_size("gy")
    my_row = lax.axis_index("gy")
    x_first = lax.axis_index("gx") * width_x - 2
    y_first = my_row * width_y - 2
    packed = jnp.concatenate(
        [marker_cells.astype(jnp.float32), marker_offset, marker_force], axis=1
    )
    slots = column_size * CAP
    column = lax.all_gather(packed, "gy", axis=0, tiled=True)
    owner_row = column[:, 1, 0].astype(jnp.int32) // width_y
    is_mine = owner_row == my_row
    chosen = jnp.argsort(jnp.where(is_mine, 0, 1), stable=True)[:slots]
    kept_flag = is_mine[chosen].astype(jnp.float32)
    received = column[chosen] * kept_flag[:, None, None]
    grouped = received.reshape(-1, group_slots, received.shape[1], markers)
    x_rows = width_x + 4
    y_rows = width_y + 4

    def spread_group(total, group):
        forces, x_matrix, y_matrix, z_matrix = slot_matrices(
            group, x_first, y_first, x_rows, y_rows, depth
        )
        lifted = (
            forces[:, None, None, :] * z_matrix[None, :, None, :] * x_matrix[None, None, :, :]
        ).astype(jnp.bfloat16)
        lifted = lifted.reshape(-1, lifted.shape[-1])
        product = lax.dot_general(
            lifted, y_matrix, (((1,), (1,)), ((), ())), preferred_element_type=jnp.float32
        )
        return (total + product, None)

    spread_init = jnp.zeros((3 * depth * x_rows, y_rows), jnp.float32)
    spread_sum, _ = lax.scan(spread_group, spread_init, grouped)
    force_padded = spread_sum.reshape(3, depth, x_rows, y_rows)
    gathered_ghosts = padded_2(force_padded, (("gx", 2), ("gy", 3)), 2)
    force_field = fold_ghosts(fold_ghosts(gathered_ghosts, 2, width_x), 3, width_y)
    lifted_visc = viscosity[None]
    padded_field, padded_visc = (
        padded_2(velocity, (("gx", 2), ("gy", 3)), 1),
        padded_2(lifted_visc, (("gx", 2), ("gy", 3)), 1),
    )
    first_field = relax(padded_field, padded_visc)
    refreshed = padded_2(first_field, (("gx", 2), ("gy", 3)), 1)
    second_field = relax(refreshed, padded_visc)
    final_field = second_field + force_field
    rim_field = padded_2(final_field.astype(jnp.bfloat16), (("gx", 2), ("gy", 3)), 2)
    rounded_flat = rim_field.reshape(-1, y_rows)

    def sample_group(carry, group):
        unused_forces, x_matrix, y_matrix, z_matrix = slot_matrices(
            group, x_first, y_first, x_rows, y_rows, depth
        )
        along_y = jnp.dot(rounded_flat, y_matrix, preferred_element_type=jnp.float32)
        along_y = along_y.reshape(3, depth, x_rows, -1)
        values = jnp.sum(
            along_y * z_matrix[None, :, None, :] * x_matrix[None, None, :, :], axis=(1, 2)
        )
        return (carry, jnp.moveaxis(values.reshape(3, group_slots, markers), 0, 1))

    _, sampled = lax.scan(sample_group, jnp.zeros((), jnp.float32), grouped)
    sampled = sampled.reshape(slots, 3, markers)
    spread_back = (
        jnp.zeros((column.shape[0], 3, markers), jnp.float32)
        .at[chosen]
        .add(sampled * kept_flag[:, None, None])
    )
    marker_velocity = lax.psum_scatter(spread_back, "gy", scatter_dimension=0, tiled=True)
    return (final_field, marker_velocity)


def solution(mesh):
    in_specs = (
        P(None, None, "gx", "gy"),
        P(None, "gx", "gy"),
        P(("gx", "gy"), None, None),
        P(("gx", "gy"), None, None),
        P(("gx", "gy"), None, None),
    )
    out_specs = (P(None, None, "gx", "gy"), P(("gx", "gy"), None, None))
    return jax.shard_map(body, mesh=mesh, in_specs=in_specs, out_specs=out_specs, check_vma=False)
```

profile of v0, /device:TPU:1, one launch (start us, length us, event | category | flops | bytes accessed | tf_op | source)
XLA Modules:
  0.0 853.1 jit_solution(3252362983962150139)
XLA Ops:
  52.5 28.9 %all-gather.2.cloned.1.call-done = f32[1024,9,128]{2,0,1:T(8,128)} async-done(((f32[32,9,128]{2,0,1:T(8,128)}), f32[1024,9,128]{2,0,1:T(8,128)}) %all-gather.2.cloned.1.call-update) | async-done | bytes 4718608 | tf_op jit(solution)/shard_map/all_gather | solution.py:99
  87.0 8.6 %copy.27 = f32[1024,9,128]{2,1,0:T(8,128)} copy(f32[1024,9,128]{2,0,1:T(8,128)} %all-gather.2.cloned.1.call-done) | data formatting | bytes 9437184 | tf_op jit(solution)/shard_map/all_gather | solution.py:99
  101.4 98.2 %while.22 = (s32[]{:T(128)}, f32[1920,132]{0,1:T(8,128)S(1)}, f32[16,4,9,128]{3,1,2,0:T(4,128)}, s32[]{:T(128)}, s32[]{:T(128)}, /*index=5*/s32[]{:T(128)}, s32[]{:T(128)}) while((s32[]{:T(128)}, f32[1920,132]{0,1:T(8,128)S(1)}, f32[16,4,9,128]{3,1,2,0:T(4,128)}, s32[]{:T(128)}, s32[]{:T(128)}, /*index=5*/s32[]{:T(128)}, ...), condition=%wide.region_2.3_spmd.clone, body=%wide.region_1.2_spmd.clone.sunk | while | flops 263266304 | bytes 10688619 | solution.py:123
  256.5 8.9 %collective-permute-start.19 = (bf16[3,32,20,2]{1,3,2,0:T(2,128)(2,1)S(1)}, bf16[3,32,20,2]{1,3,2,0:T(2,128)(2,1)S(1)}, u32[]{:S(2)}, u32[]{:S(2)}) collective-permute-start(bf16[3,32,20,2]{1,3,2,0:T(2,128)(2,1)S(1)} %copy.35), channel_id=1, source_target_pairs={{1,0},{2,1},{3,2},{4,3},{5,4},{6,5},{7,6},{8,7},{9,8},{10,9},{11,1... | collective-permute-start | bytes 23048 | tf_op jit(solution)/shard_map/ppermute | solution.py:19
  272.0 275.1 %while.21 = (s32[]{:T(128)}, f32[16,4,3,128]{3,2,1,0:T(4,128)S(1)}, f32[16,4,9,128]{3,1,2,0:T(4,128)}, s32[]{:T(128)}, bf16[1920,132]{1,0:T(8,128)(2,1)S(1)}, /*index=5*/s32[]{:T(128)}, s32[]{:T(128)}) while((s32[]{:T(128)}, f32[16,4,3,128]{3,2,1,0:T(4,128)S(1)}, f32[16,4,9,128]{3,1,2,0:T(4,128)}, s32[]{:T(128)}, ...), condition=%wide.region_5.6_spmd, body=%wide.region_3.5_spmd.sunk | while | flops 263691776 | bytes 24585316 | solution.py:150
  275.6 5.6 copy.51
  281.2 4.9 reshape.1370
  292.8 5.6 copy.51
  298.4 4.9 reshape.1370
  310.0 5.6 copy.51
  315.5 4.9 reshape.1370
  327.2 5.6 copy.51
  344.4 5.6 copy.51
  361.6 5.6 copy.51
  367.1 4.9 reshape.1370
  378.8 5.6 copy.51
  396.0 5.6 copy.51
  401.5 4.9 reshape.1370
  413.2 5.6 copy.51
  418.7 4.9 reshape.1370
  430.4 5.6 copy.51
  435.9 4.9 reshape.1370
  447.6 5.6 copy.51
  453.1 4.9 reshape.1370
  464.8 5.6 copy.51
  470.3 4.9 reshape.1370
  481.9 5.6 copy.51
  487.5 4.9 reshape.1370
  499.1 5.6 copy.51
  516.3 5.6 copy.51
  533.5 5.6 copy.51
  553.0 291.5 %all-reduce.7.cloned.1.call-done = f32[1024,3,128]{2,1,0:T(4,128)} async-done(((f32[1024,3,128]{2,1,0:T(4,128)}), f32[1024,3,128]{2,1,0:T(4,128)}) %all-reduce.7.cloned.1.call-update) | async-done | bytes 1572880
  (616 shorter events, 359.2 us)
Async XLA Ops:
  7.2 14.2 %copy-start.4 = (f32[3,32,16,128]{3,2,1,0:T(8,128)S(1)}, f32[3,32,16,128]{3,2,1,0:T(8,128)}, u32[]{:S(2)}) copy-start(f32[3,32,16,128]{3,2,1,0:T(8,128)} %param.9) | copy-start | bytes 2359300
  7.2 74.2 %all-gather.2.cloned.1.call-start = ((), (), s32[]{:S(2)}) async-start(), calls=%async_computation | async-start | bytes 4866048 | tf_op jit(solution)/shard_map/all_gather | solution.py:99
  9.6 834.9 %all-reduce.7.cloned.1.call-start = ((), (), s32[]{:S(2)}) async-start(), calls=%async_computation.1 | async-start | bytes 4194304
  10.8 19.0 %collective-permute-start.3 = (f32[3,32,1,128]{3,2,1,0:T(1,128)S(1)}, f32[3,32,1,128]{3,2,1,0:T(1,128)S(1)}, u32[]{:S(2)}, u32[]{:S(2)}) collective-permute-start(f32[3,32,1,128]{3,2,1,0:T(1,128)S(1)} %get-tuple-element.206), channel_id=1, source_target_pairs={{32,0},{64,32},{96,64},{128,96},{160,128},{192,160},{224,192},{0,2... | collective-permute-start | bytes 147464 | tf_op jit(solution)/shard_map/ppermute | solution.py:19
  15.6 14.3 %collective-permute-start.1 = (f32[3,32,1,128]{3,2,1,0:T(1,128)S(1)}, f32[3,32,1,128]{3,2,1,0:T(1,128)S(1)}, u32[]{:S(2)}, u32[]{:S(2)}) collective-permute-start(f32[3,32,1,128]{3,2,1,0:T(1,128)S(1)} %get-tuple-element.205), channel_id=1, source_target_pairs={{0,32},{32,64},{64,96},{96,128},{128,160},{160,192},{192,224},{224... | collective-permute-start | bytes 147464 | tf_op jit(solution)/shard_map/ppermute | solution.py:18
  16.6 4.9 collective-permute-start.2
  20.2 4.7 copy-start.10
  20.2 4.7 collective-permute-start
  26.0 12.5 %collective-permute-start.4 = (f32[1,32,18,1]{3,2,1,0:T(8,128)}, f32[1,32,18,1]{3,2,1,0:T(8,128)S(1)}, u32[]{:S(2)}, u32[]{:S(2)}) collective-permute-start(f32[1,32,18,1]{3,2,1,0:T(8,128)} %get-tuple-element.211), channel_id=1, source_target_pairs={{0,1},{1,2},{2,3},{3,4},{4,5},{5,6},{6,7},{7,8},{8,9},{9,10},{10,1... | collective-permute-start | bytes 6920 | tf_op jit(solution)/shard_map/ppermute | solution.py:18
  29.8 8.7 %collective-permute-start.6 = (f32[1,32,18,1]{3,2,1,0:T(8,128)}, f32[1,32,18,1]{3,2,1,0:T(8,128)}, u32[]{:S(2)}, u32[]{:S(2)}) collective-permute-start(f32[1,32,18,1]{3,2,1,0:T(8,128)} %get-tuple-element.212), channel_id=1, source_target_pairs={{1,0},{2,1},{3,2},{4,3},{5,4},{6,5},{7,6},{8,7},{9,8},{10,9},{11,1... | collective-permute-start | bytes 6920 | tf_op jit(solution)/shard_map/ppermute | solution.py:19
  33.1 7.7 collective-permute-start.7
  38.4 2.9 collective-permute-start.5
  45.5 35.8 %copy-start = (f32[3,32,16,128]{3,2,1,0:T(8,128)}, f32[3,32,16,128]{3,2,1,0:T(8,128)S(1)}, u32[]{:S(2)}) copy-start(f32[3,32,16,128]{3,2,1,0:T(8,128)S(1)} %fusion.220) | copy-start | bytes 2359300
  45.6 3.3 collective-permute-start.9
  45.8 5.5 collective-permute-start.8
  49.0 46.7 %copy-start.18 = (f32[3,32,1,128]{3,2,1,0:T(1,128)}, f32[3,32,1,128]{3,2,1,0:T(1,128)S(1)}, u32[]{:S(2)}) copy-start(f32[3,32,1,128]{3,2,1,0:T(1,128)S(1)} %collective-permute-done.9) | copy-start | bytes 147460
  51.3 44.3 %copy-start.20 = (f32[3,32,1,128]{3,2,1,0:T(1,128)}, f32[3,32,1,128]{3,2,1,0:T(1,128)S(1)}, u32[]{:S(2)}) copy-start(f32[3,32,1,128]{3,2,1,0:T(1,128)S(1)} %collective-permute-done.8) | copy-start | bytes 147460
  201.5 4.3 copy-start.5
  204.1 8.6 %collective-permute-start.13 = (f32[3,32,2,132]{3,2,1,0:T(2,128)}, f32[3,32,2,132]{3,2,1,0:T(2,128)}, u32[]{:S(2)}, u32[]{:S(2)}) collective-permute-start(f32[3,32,2,132]{3,2,1,0:T(2,128)} %get-tuple-element.196), channel_id=1, source_target_pairs={{32,0},{64,32},{96,64},{128,96},{160,128},{192,160},{224,192},{0,2... | collective-permute-start | bytes 304136 | tf_op jit(solution)/shard_map/ppermute | solution.py:19
  205.8 8.4 collective-permute-start.12
  207.6 3.0 copy-start.9
  210.0 15.0 %collective-permute-start.11 = (f32[3,32,18,1]{1,3,2,0:T(1,128)}, f32[3,32,18,1]{1,3,2,0:T(1,128)}, u32[]{:S(2)}, u32[]{:S(2)}) collective-permute-start(f32[3,32,18,1]{1,3,2,0:T(1,128)} %copy.25), channel_id=1, source_target_pairs={{1,0},{2,1},{3,2},{4,3},{5,4},{6,5},{7,6},{8,7},{9,8},{10,9},{11,1... | collective-permute-start | bytes 20744 | tf_op jit(solution)/shard_map/ppermute | solution.py:19
  211.7 15.6 %collective-permute-start.10 = (f32[3,32,18,1]{1,3,2,0:T(1,128)}, f32[3,32,18,1]{1,3,2,0:T(1,128)}, u32[]{:S(2)}, u32[]{:S(2)}) collective-permute-start(f32[3,32,18,1]{1,3,2,0:T(1,128)} %copy.23), channel_id=1, source_target_pairs={{0,1},{1,2},{2,3},{3,4},{4,5},{5,6},{6,7},{7,8},{8,9},{9,10},{10,1... | collective-permute-start | bytes 20744 | tf_op jit(solution)/shard_map/ppermute | solution.py:18
  217.5 6.6 copy-start.1
  217.5 6.6 copy-start.17
  219.3 10.2 %collective-permute-start.15 = (f32[3,32,24,2]{1,2,3,0:T(8,128)S(1)}, f32[3,32,24,2]{1,2,3,0:T(8,128)S(1)}, u32[]{:S(2)}, u32[]{:S(2)}) collective-permute-start(f32[3,32,24,2]{1,2,3,0:T(8,128)S(1)} %copy.31), channel_id=1, source_target_pairs={{1,0},{2,1},{3,2},{4,3},{5,4},{6,5},{7,6},{8,7},{9,8},{10,9},{11,1... | collective-permute-start | bytes 55304 | tf_op jit(solution)/shard_map/ppermute | solution.py:19
  223.3 7.8 collective-permute-start.14
  247.8 3.8 collective-permute-start.17
  250.4 5.0 collective-permute-start.16
  256.5 9.8 %collective-permute-start.19 = (bf16[3,32,20,2]{1,3,2,0:T(2,128)(2,1)S(1)}, bf16[3,32,20,2]{1,3,2,0:T(2,128)(2,1)S(1)}, u32[]{:S(2)}, u32[]{:S(2)}) collective-permute-start(bf16[3,32,20,2]{1,3,2,0:T(2,128)(2,1)S(1)} %copy.35), channel_id=1, source_target_pairs={{1,0},{2,1},{3,2},{4,3},{5,4},{6,5},{7,6},{8,7},{9,8},{10,9},{11,1... | collective-permute-start | bytes 23048 | tf_op jit(solution)/shard_map/ppermute | solution.py:19
  265.9 4.0 collective-permute-start.18
  547.6 4.1 copy-start.24
  (15 other events, 21.9 us)
Sparse Core Ops, SparseCore 0:
  10.6 70.7 all-gather.1
  551.8 292.6 all-reduce.6
where the time goes:
time: 868 us; the launch traced here: 853 us
  waiting for transfers between devices  337 us (39%)
  local copies, waits for them, and re-layouts  279 us (32%)
  other arithmetic  99.6 us (11%)
  matrix products  82.7 us (10%)
  starting transfers between devices  36.6 us (4%)
  between operations  15.4 us (2%)
    unnamed x3, waiting for transfers between devices  292 us
    dot_general x16, local copies, waits for them, and re-layouts, sample_group(): jnp.dot(rounded_flat, y_matrix, preferred_element_type=jnp.float32)  88.9 us
    reshape x16, local copies, waits for them, and re-layouts, sample_group(): along_y = along_y.reshape(3, depth, x_rows, -1)  77.9 us
    reduce_sum x16, other arithmetic, sample_group(): jnp.sum(along_y * z_matrix[None, :, None, :] * x_matrix[None, None, :, :]...  48.3 us
    dot_general x16, matrix products, sample_group(): jnp.dot(rounded_flat, y_matrix, preferred_element_type=jnp.float32)  43.1 us
    dot_general x16, matrix products, spread_group(): lax.dot_general(lifted, y_matrix, (((1,), (1,)), ((), ())), preferred_ele...  39.6 us
    convert_element_type x16, local copies, waits for them, and re-layouts, spread_group(): lifted = (forces[:, None, None, :] * z_matrix[None, :, None, :] * x_matri...  31.8 us
    ppermute x10, starting transfers between devices, padded_2(): after = lax.ppermute(first, axis, down)  28.9 us
  transfers between devices with their start and end apart: 22, of which 11 were waited for; matrix products, arithmetic and copies ran while one was open for 4% of the time, Pallas kernels for 0%

commit v1 on v0

--- a/solution.py
+++ b/solution.py
@@ -6,6 +6,11 @@
 CAP = 2
 OFFSETS = (-1, 0, 1, 2)
 group_slots = 4
+
+
+def swapped_in(block, name, dim):
+    sent = jnp.stack([block] * lax.axis_size(name))
+    return jnp.concatenate(lax.all_to_all(sent, name, 0, 0), axis=dim)
 
 
 def padded_2(array, sides, width):
@@ -96,7 +101,7 @@
         [marker_cells.astype(jnp.float32), marker_offset, marker_force], axis=1
     )
     slots = column_size * CAP
-    column = lax.all_gather(packed, "gy", axis=0, tiled=True)
+    column = swapped_in(packed, "gy", 0)
     owner_row = column[:, 1, 0].astype(jnp.int32) // width_y
     is_mine = owner_row == my_row
     chosen = jnp.argsort(jnp.where(is_mine, 0, 1), stable=True)[:slots]

time: 868 us -> 951 us (1.096)
  waiting for transfers between devices: 337 us -> 404 us
  starting transfers between devices: 36.6 us -> 53.4 us
    ppermute x10, waiting for transfers between devices: 2.89 us -> 96.5 us  [padded_2(): after = lax.ppermute(first, axis, down)]
    all_gather x1 -> x0, waiting for transfers between devices: 28.9 us -> none  [body(): column = lax.all_gather(packed, 'gy', axis=0, tiled=True)]
    all_to_all x0 -> x1, starting transfers between devices: none -> 12.9 us  [swapped_in(): return jnp.concatenate(lax.all_to_all(sent, name, 0, 0), axis=dim)]
    unnamed x3 -> x2, waiting for transfers between devices: 292 us -> 292 us
  transfers between devices with their start and end apart: 22 -> 22, of which waited for: 11 -> 9; matrix products, arithmetic and copies ran while one was open for 4% -> 4% of each run, Pallas kernels for 0% -> 0%
where the time goes in v1:
time: 951 us; the launch traced here: 935 us
  waiting for transfers between devices  404 us (42%)
  local copies, waits for them, and re-layouts  280 us (29%)
  other arithmetic  96.7 us (10%)
  matrix products  82.9 us (9%)
  starting transfers between devices  53.4 us (6%)
  between operations  15.5 us (2%)
    unnamed x2, waiting for transfers between devices  292 us
    ppermute x10, waiting for transfers between devices, padded_2(): after = lax.ppermute(first, axis, down)  96.5 us
    dot_general x16, local copies, waits for them, and re-layouts, sample_group(): jnp.dot(rounded_flat, y_matrix, preferred_element_type=jnp.float32)  89 us
    reshape x16, local copies, waits for them, and re-layouts, sample_group(): along_y = along_y.reshape(3, depth, x_rows, -1)  77.9 us
    reduce_sum x16, other arithmetic, sample_group(): jnp.sum(along_y * z_matrix[None, :, None, :] * x_matrix[None, None, :, :]...  48.3 us
    dot_general x16, matrix products, sample_group(): jnp.dot(rounded_flat, y_matrix, preferred_element_type=jnp.float32)  43.2 us
    dot_general x16, matrix products, spread_group(): lax.dot_general(lifted, y_matrix, (((1,), (1,)), ((), ())), preferred_ele...  39.7 us
    ppermute x10, starting transfers between devices, padded_2(): after = lax.ppermute(first, axis, down)  34.7 us
  transfers between devices with their start and end apart: 22, of which 9 were waited for; matrix products, arithmetic and copies ran while one was open for 4% of the time, Pallas kernels for 0%

profile of v1, /device:TPU:1, one launch (start us, length us, event | category | flops | bytes accessed | tf_op | source)
XLA Modules:
  0.0 935.5 jit_solution(15718769690185865104)
XLA Ops:
  11.6 12.9 %all-to-all-start = ((f32[32,32,9,128]{3,1,2,0:T(8,128)}), f32[32,32,9,128]{3,1,2,0:T(8,128)}, u32[]{:S(2)}, u32[]{:S(2)}) async-start(f32[32,32,9,128]{3,1,2,0:T(8,128)} %stack.2), calls=%async_computation | async-start | bytes 9437184 | tf_op jit(solution)/shard_map/all_to_all | solution.py:13
  31.5 94.2 %collective-permute-done.2 = f32[1,32,1,128]{3,2,1,0:T(1,128)S(1)} collective-permute-done((f32[1,32,1,128]{3,2,1,0:T(1,128)S(1)}, f32[1,32,1,128]{3,2,1,0:T(1,128)S(1)}, u32[]{:S(2)}, u32[]{:S(2)}) %collective-permute-start.2) | collective-permute-done | bytes 16416 | tf_op jit(solution)/shard_map/ppermute | solution.py:24
  125.7 5.4 collective-permute-done
  159.4 6.3 copy.32
  176.1 98.4 %while.22 = (s32[]{:T(128)}, f32[1920,132]{0,1:T(8,128)S(1)}, f32[16,4,9,128]{3,1,0,2:T(4,128)}, s32[]{:T(128)}, s32[]{:T(128)}, /*index=5*/s32[]{:T(128)}, s32[]{:T(128)}) while((s32[]{:T(128)}, f32[1920,132]{0,1:T(8,128)S(1)}, f32[16,4,9,128]{3,1,0,2:T(4,128)}, s32[]{:T(128)}, s32[]{:T(128)}, /*index=5*/s32[]{:T(128)}, ...), condition=%wide.region_2.3_spmd.clone, body=%wide.region_1.2_spmd.clone.sunk | while | flops 263266304 | bytes 10688619 | solution.py:128
  284.7 7.9 collective-permute-start.11
  338.2 8.7 collective-permute-start.19
  353.5 275.3 %while.21 = (s32[]{:T(128)}, f32[16,4,3,128]{3,2,1,0:T(4,128)S(1)}, f32[16,4,9,128]{3,1,0,2:T(4,128)}, s32[]{:T(128)}, bf16[1920,132]{1,0:T(8,128)(2,1)S(1)}, /*index=5*/s32[]{:T(128)}, s32[]{:T(128)}) while((s32[]{:T(128)}, f32[16,4,3,128]{3,2,1,0:T(4,128)S(1)}, f32[16,4,9,128]{3,1,0,2:T(4,128)}, s32[]{:T(128)}, ...), condition=%wide.region_5.6_spmd, body=%wide.region_3.5_spmd.sunk | while | flops 263691776 | bytes 24585316 | solution.py:155
  357.1 5.6 copy.57
  362.7 4.9 reshape.1376
  374.3 5.6 copy.57
  391.5 5.6 copy.57
  397.1 4.9 reshape.1376
  408.7 5.6 copy.57
  425.9 5.6 copy.57
  431.5 4.9 reshape.1376
  443.2 5.6 copy.57
  460.4 5.6 copy.57
  465.9 4.9 reshape.1376
  477.6 5.6 copy.57
  494.8 5.6 copy.57
  512.0 5.6 copy.57
  529.2 5.6 copy.57
  546.4 5.6 copy.57
  552.0 4.9 reshape.1376
  563.6 5.6 copy.57
  580.8 5.6 copy.57
  586.4 4.9 reshape.1376
  598.0 5.6 copy.57
  615.2 5.6 copy.57
  620.8 4.9 reshape.1376
  634.7 292.2 %all-reduce.7.cloned.1.call-done = f32[1024,3,128]{2,1,0:T(4,128)} async-done(((f32[1024,3,128]{2,1,0:T(4,128)}), f32[1024,3,128]{2,1,0:T(4,128)}) %all-reduce.7.cloned.1.call-update) | async-done | bytes 1572880
  (618 shorter events, 366.3 us)
Async XLA Ops:
  11.6 13.0 %copy-start.4 = (f32[3,32,16,128]{3,2,1,0:T(8,128)S(1)}, f32[3,32,16,128]{3,2,1,0:T(8,128)}, u32[]{:S(2)}) copy-start(f32[3,32,16,128]{3,2,1,0:T(8,128)} %param.9) | copy-start | bytes 2359300
  11.6 16.1 %copy-start.10 = (f32[32,16,128]{2,1,0:T(8,128)S(1)}, f32[32,16,128]{2,1,0:T(8,128)}, u32[]{:S(2)}) copy-start(f32[32,16,128]{2,1,0:T(8,128)} %param.10) | copy-start | bytes 786436
  11.6 144.9 %all-to-all-start = ((f32[32,32,9,128]{3,1,2,0:T(8,128)}), f32[32,32,9,128]{3,1,2,0:T(8,128)}, u32[]{:S(2)}, u32[]{:S(2)}) async-start(f32[32,32,9,128]{3,1,2,0:T(8,128)} %stack.2), calls=%async_computation | async-start | bytes 9437184 | tf_op jit(solution)/shard_map/all_to_all | solution.py:13
  24.5 902.4 %all-reduce.7.cloned.1.call-start = ((), (), s32[]{:S(2)}) async-start(), calls=%async_computation.1 | async-start | bytes 4194304
  24.7 109.4 %collective-permute-start.3 = (f32[3,32,1,128]{3,2,1,0:T(1,128)S(1)}, f32[3,32,1,128]{3,2,1,0:T(1,128)S(1)}, u32[]{:S(2)}, u32[]{:S(2)}) collective-permute-start(f32[3,32,1,128]{3,2,1,0:T(1,128)S(1)} %get-tuple-element.224), channel_id=1, source_target_pairs={{32,0},{64,32},{96,64},{128,96},{160,128},{192,160},{224,192},{0,2... | collective-permute-start | bytes 147464 | tf_op jit(solution)/shard_map/ppermute | solution.py:24
  27.7 106.4 %collective-permute-start.1 = (f32[3,32,1,128]{3,2,1,0:T(1,128)S(1)}, f32[3,32,1,128]{3,2,1,0:T(1,128)S(1)}, u32[]{:S(2)}, u32[]{:S(2)}) collective-permute-start(f32[3,32,1,128]{3,2,1,0:T(1,128)S(1)} %get-tuple-element.223), channel_id=1, source_target_pairs={{0,32},{32,64},{64,96},{96,128},{128,160},{160,192},{192,224},{224... | collective-permute-start | bytes 147464 | tf_op jit(solution)/shard_map/ppermute | solution.py:23
  27.7 98.0 %collective-permute-start.2 = (f32[1,32,1,128]{3,2,1,0:T(1,128)S(1)}, f32[1,32,1,128]{3,2,1,0:T(1,128)S(1)}, u32[]{:S(2)}, u32[]{:S(2)}) collective-permute-start(f32[1,32,1,128]{3,2,1,0:T(1,128)S(1)} %get-tuple-element.236), channel_id=1, source_target_pairs={{32,0},{64,32},{96,64},{128,96},{160,128},{192,160},{224,192},{0,2... | collective-permute-start | bytes 49160 | tf_op jit(solution)/shard_map/ppermute | solution.py:24
  31.4 99.8 %collective-permute-start = (f32[1,32,1,128]{3,2,1,0:T(1,128)S(1)}, f32[1,32,1,128]{3,2,1,0:T(1,128)S(1)}, u32[]{:S(2)}, u32[]{:S(2)}) collective-permute-start(f32[1,32,1,128]{3,2,1,0:T(1,128)S(1)} %get-tuple-element.235), channel_id=1, source_target_pairs={{0,32},{32,64},{64,96},{96,128},{128,160},{160,192},{192,224},{224... | collective-permute-start | bytes 49160 | tf_op jit(solution)/shard_map/ppermute | solution.py:23
  31.4 94.3 %copy-start.16 = (f32[31,16,128]{2,1,0:T(8,128)}, f32[31,16,128]{2,1,0:T(8,128)S(1)}, u32[]{:S(2)}) copy-start(f32[31,16,128]{2,1,0:T(8,128)S(1)} %fusion.244) | copy-start | bytes 761860
  132.2 10.3 %collective-permute-start.4 = (f32[1,32,18,1]{3,2,1,0:T(8,128)}, f32[1,32,18,1]{3,2,1,0:T(8,128)S(1)}, u32[]{:S(2)}, u32[]{:S(2)}) collective-permute-start(f32[1,32,18,1]{3,2,1,0:T(8,128)} %get-tuple-element.229), channel_id=1, source_target_pairs={{0,1},{1,2},{2,3},{3,4},{4,5},{5,6},{6,7},{7,8},{8,9},{9,10},{10,1... | collective-permute-start | bytes 6920 | tf_op jit(solution)/shard_map/ppermute | solution.py:23
  134.1 8.5 collective-permute-start.6
  137.3 7.5 collective-permute-start.7
  142.4 2.9 collective-permute-start.5
  149.5 9.9 %copy-start = (f32[3,32,16,128]{3,2,1,0:T(8,128)}, f32[3,32,16,128]{3,2,1,0:T(8,128)S(1)}, u32[]{:S(2)}) copy-start(f32[3,32,16,128]{3,2,1,0:T(8,128)S(1)} %fusion.220) | copy-start | bytes 2359300
  149.6 3.0 collective-permute-start.9
  149.7 5.6 collective-permute-start.8
  152.6 6.8 copy-start.18
  155.3 4.1 copy-start.20
  279.1 14.7 %collective-permute-start.13 = (f32[3,32,2,132]{3,2,1,0:T(2,128)}, f32[3,32,2,132]{3,2,1,0:T(2,128)}, u32[]{:S(2)}, u32[]{:S(2)}) collective-permute-start(f32[3,32,2,132]{3,2,1,0:T(2,128)} %get-tuple-element.214), channel_id=1, source_target_pairs={{32,0},{64,32},{96,64},{128,96},{160,128},{192,160},{224,192},{0,2... | collective-permute-start | bytes 304136 | tf_op jit(solution)/shard_map/ppermute | solution.py:24
  279.1 14.7 %collective-permute-start.12 = (f32[3,32,2,132]{3,2,1,0:T(2,128)}, f32[3,32,2,132]{3,2,1,0:T(2,128)}, u32[]{:S(2)}, u32[]{:S(2)}) collective-permute-start(f32[3,32,2,132]{3,2,1,0:T(2,128)} %get-tuple-element.213), channel_id=1, source_target_pairs={{0,32},{32,64},{64,96},{96,128},{128,160},{160,192},{192,224},{224... | collective-permute-start | bytes 304136 | tf_op jit(solution)/shard_map/ppermute | solution.py:23
  282.3 10.3 %copy-start.9 = (f32[3,32,18,1]{3,2,1,0:T(8,128)S(1)}, f32[3,32,18,1]{3,2,1,0:T(8,128)}, u32[]{:S(2)}) copy-start(f32[3,32,18,1]{3,2,1,0:T(8,128)} %get-tuple-element.217) | copy-start | bytes 20740
  284.7 22.1 %collective-permute-start.11 = (f32[3,32,18,1]{1,3,2,0:T(1,128)}, f32[3,32,18,1]{1,3,2,0:T(1,128)}, u32[]{:S(2)}, u32[]{:S(2)}) collective-permute-start(f32[3,32,18,1]{1,3,2,0:T(1,128)} %copy.29), channel_id=1, source_target_pairs={{1,0},{2,1},{3,2},{4,3},{5,4},{6,5},{7,6},{8,7},{9,8},{10,9},{11,1... | collective-permute-start | bytes 20744 | tf_op jit(solution)/shard_map/ppermute | solution.py:24
  293.6 15.4 %collective-permute-start.10 = (f32[3,32,18,1]{1,3,2,0:T(1,128)}, f32[3,32,18,1]{1,3,2,0:T(1,128)}, u32[]{:S(2)}, u32[]{:S(2)}) collective-permute-start(f32[3,32,18,1]{1,3,2,0:T(1,128)} %copy.27), channel_id=1, source_target_pairs={{0,1},{1,2},{2,3},{3,4},{4,5},{5,6},{6,7},{7,8},{8,9},{9,10},{10,1... | collective-permute-start | bytes 20744 | tf_op jit(solution)/shard_map/ppermute | solution.py:23
  297.1 8.7 copy-start.1
  297.1 8.7 copy-start.17
  298.9 12.4 %collective-permute-start.15 = (f32[3,32,24,2]{1,2,3,0:T(8,128)S(1)}, f32[3,32,24,2]{1,2,3,0:T(8,128)S(1)}, u32[]{:S(2)}, u32[]{:S(2)}) collective-permute-start(f32[3,32,24,2]{1,2,3,0:T(8,128)S(1)} %copy.37), channel_id=1, source_target_pairs={{1,0},{2,1},{3,2},{4,3},{5,4},{6,5},{7,6},{8,7},{9,8},{10,9},{11,1... | collective-permute-start | bytes 55304 | tf_op jit(solution)/shard_map/ppermute | solution.py:24
  305.8 7.1 collective-permute-start.14
  329.7 3.4 collective-permute-start.17
  331.9 5.2 collective-permute-start.16
  338.2 9.5 %collective-permute-start.19 = (bf16[3,32,20,2]{1,3,2,0:T(2,128)(2,1)S(1)}, bf16[3,32,20,2]{1,3,2,0:T(2,128)(2,1)S(1)}, u32[]{:S(2)}, u32[]{:S(2)}) collective-permute-start(bf16[3,32,20,2]{1,3,2,0:T(2,128)(2,1)S(1)} %copy.41), channel_id=1, source_target_pairs={{1,0},{2,1},{3,2},{4,3},{5,4},{6,5},{7,6},{8,7},{9,8},{10,9},{11,1... | collective-permute-start | bytes 23048 | tf_op jit(solution)/shard_map/ppermute | solution.py:24
  347.3 4.1 collective-permute-start.18
  629.0 4.4 copy-start.24
  (15 other events, 25.8 us)
Sparse Core Ops, SparseCore 0:
  633.5 293.3 all-reduce.6
